TPU v7x, 32 devices: a whole 2x2x4 slice. The times are simulated.
32 devices in a mesh: wide: 16 (over z, y, core), narrow: 2 (over x).
Axes of the slice: x: 2, y: 2, z: 4, core: 2. Of those that a mesh axis runs over, the one named last changes fastest.
Arguments:
- inputs: bfloat16 [2, 32, 128, 1024], P(None, ('wide', 'narrow')), may hold values from -6 to 6
- out_grad: bfloat16 [2, 32, 128, 1024], P(None, ('wide', 'narrow')), may hold values from -6 to 6
- group_id: int32 [2, 32], P(None, ('wide', 'narrow')), may hold values from 0 to 15
- group_count: int32 [16], replicated, may hold values from 1 to 4
- norm_gain: bfloat16 [4, 1024], P(None, 'narrow'), may hold values from 0.5 to 1.5
- norm_bias: bfloat16 [4, 1024], P(None, 'narrow'), may hold values from -1.25 to 1.25
- w_qkv: bfloat16 [1024, 3072], P('narrow'), may hold values from -0.1875 to 0.1875
- w_out: bfloat16 [1024, 1024], P('narrow'), may hold values from -1.5 to 1.5
- w_up: bfloat16 [1024, 4096], P('narrow'), may hold values from -0.1875 to 0.1875
- w_down: bfloat16 [4096, 1024], P('narrow'), may hold values from -0.09375 to 0.09375
- bias_model: bfloat16 [4, 1024], P(None, 'narrow'), may hold values from -0.625 to 0.625
- bias_up: bfloat16 [4096], P('narrow'), may hold values from -0.625 to 0.625
Outputs:
- output: bfloat16 [2, 32, 128, 1024], P(None, ('wide', 'narrow'))
- grad_input: bfloat16 [2, 32, 128, 1024], P(None, ('wide', 'narrow'))
- grad_norm_gain: float32 [4, 1024], P(None, 'narrow')
- grad_norm_bias: float32 [4, 1024], P(None, 'narrow')
- grad_qkv: float32 [1024, 3072], P('narrow')
- grad_out: float32 [1024, 1024], P('narrow')
- grad_up: float32 [1024, 4096], P('narrow')
- grad_down: float32 [4096, 1024], P('narrow')
- grad_bias_model: float32 [4, 1024], P(None, 'narrow')
- grad_bias_up: float32 [4096], P('narrow')
All inputs are finite; a program needn't handle non-finite values.
Results may differ from a plain program's by a relative error of at most 0.02.
Values may be sent and summed in bfloat16 or wider, within the bound.
No kernel may reach another device: no remote copies, remote signals or barrier semaphores. Data moves between devices by JAX's collectives and lax.ppermute only.
A program may use at most 256 MiB of HBM per device.

v0:
```python
import math
import jax
import jax.numpy as jnp
from jax import lax
from jax.sharding import PartitionSpec as P

HEADS = 16
EPSILON = 1e-05
RELAX = 32.0


def layer_norm(value, gain, shift):
    average = jnp.mean(value, axis=-1, keepdims=True)
    centred = value - average
    spread = jnp.mean(centred * centred, axis=-1, keepdims=True)
    return centred * lax.rsqrt(spread + EPSILON) * gain + shift


def exact_gelu(value):
    return jax.nn.gelu(value, approximate=False)


def forward_product(left, right):
    return jnp.dot(left, right, preferred_element_type=jnp.float32)


def back_product(grad, weight):
    return lax.dot_general(
        grad, weight, (((1,), (1,)), ((), ())), preferred_element_type=jnp.float32
    )


def weight_grad(left, grad):
    return lax.dot_general(left, grad, (((0,), (0,)), ((), ())), preferred_element_type=jnp.float32)


def column_sum(grad):
    return jnp.sum(grad.astype(jnp.float32), axis=0)


def split_heads(qkv, seqs, heads):
    length = qkv.shape[0] // seqs
    width = qkv.shape[1] // 3
    parts = qkv.reshape(seqs, length, 3, heads, width // heads)
    return (parts[:, :, 0], parts[:, :, 1], parts[:, :, 2])


def raw_scores(query, keys):
    length = query.shape[1]
    scale = RELAX * math.sqrt(query.shape[-1])
    scores = jnp.einsum("sqhd,skhd->shqk", query, keys, preferred_element_type=jnp.float32) / scale
    rows = lax.broadcasted_iota(jnp.int32, (length, length), 0)
    columns = lax.broadcasted_iota(jnp.int32, (length, length), 1)
    return jnp.where(columns <= rows, scores, -1000000000.0)


def forward_pass(block, full, seqs, heads):
    gain = full[0].astype(jnp.float32)
    shift = full[1].astype(jnp.float32)
    bias = full[6].astype(jnp.float32)
    bias_hidden = full[7].astype(jnp.float32)
    tokens, width = block.shape
    qkv_bias = jnp.concatenate([bias[0], jnp.zeros((width,), jnp.float32), bias[1]])
    block_value = block.astype(jnp.float32)
    first = layer_norm(block_value, gain[0], shift[0]).astype(jnp.bfloat16)
    qkv = (forward_product(first, full[2]) + qkv_bias).astype(jnp.bfloat16)
    query, keys, values = split_heads(qkv, seqs, heads)
    scores = raw_scores(query, keys)
    top = jnp.max(scores, axis=-1, keepdims=True)
    exps = jnp.exp(RELAX * (scores - top))
    total = jnp.sum(exps, axis=-1, keepdims=True)
    logsum = jnp.log(total)
    weights = (exps / total).astype(jnp.bfloat16)
    mixed = jnp.einsum("shqk,skhd->sqhd", weights, values, preferred_element_type=jnp.float32)
    mixed = mixed.reshape(tokens, width).astype(jnp.bfloat16)
    branch = forward_product(mixed, full[3]) + bias[2]
    middle = block_value + layer_norm(branch, gain[1], shift[1])
    third = layer_norm(middle, gain[2], shift[2]).astype(jnp.bfloat16)
    hidden = forward_product(third, full[4]) + bias_hidden
    active = exact_gelu(hidden).astype(jnp.bfloat16)
    second = forward_product(active, full[5]) + bias[3]
    result = middle + layer_norm(second, gain[3], shift[3])
    kept = (
        block_value,
        first,
        qkv,
        top,
        logsum,
        mixed,
        branch,
        middle,
        third,
        hidden,
        active,
        second,
    )
    return (result, kept)


def attention_back(qkv, top, logsum, grad_mixed, seqs, heads):
    query, keys, values = split_heads(qkv, seqs, heads)
    scores = raw_scores(query, keys)
    probs = jnp.exp(RELAX * (scores - top) - logsum)
    weights = probs.astype(jnp.bfloat16)
    tokens, width = grad_mixed.shape
    grad_heads = grad_mixed.reshape(seqs, tokens // seqs, heads, width // heads)
    grad_weights = jnp.einsum(
        "sqhd,skhd->shqk", grad_heads, values, preferred_element_type=jnp.float32
    )
    inner = jnp.sum(probs * grad_weights, axis=-1, keepdims=True)
    grad_scores = (RELAX * probs * (grad_weights - inner)).astype(jnp.bfloat16)
    scale = RELAX * math.sqrt(query.shape[-1])
    grad_query = (
        jnp.einsum("shqk,skhd->sqhd", grad_scores, keys, preferred_element_type=jnp.float32) / scale
    )
    grad_keys = (
        jnp.einsum("shqk,sqhd->skhd", grad_scores, query, preferred_element_type=jnp.float32)
        / scale
    )
    grad_values = jnp.einsum(
        "shqk,sqhd->skhd", weights, grad_heads, preferred_element_type=jnp.float32
    )
    stacked = jnp.stack([grad_query, grad_keys, grad_values], axis=2)
    return stacked.reshape(tokens, 3 * width).astype(jnp.bfloat16)


def backward_pass(cotangent, full, kept, seqs, heads):
    block_value, first, qkv, top, logsum, mixed, branch, middle, third, hidden, active, second = (
        kept
    )
    gain = full[0].astype(jnp.float32)
    shift = full[1].astype(jnp.float32)
    width = block_value.shape[1]
    unused_last, pull_last = jax.vjp(layer_norm, second, gain[3], shift[3])
    grad_second, gain_last, shift_last = pull_last(cotangent)
    grad_second = grad_second.astype(jnp.bfloat16)
    grad_down = weight_grad(active, grad_second)
    bias_down = column_sum(grad_second)
    grad_active = back_product(grad_second, full[5])
    unused_gelu, pull_gelu = jax.vjp(exact_gelu, hidden)
    grad_hidden = pull_gelu(grad_active)[0].astype(jnp.bfloat16)
    grad_up = weight_grad(third, grad_hidden)
    bias_hidden = column_sum(grad_hidden)
    grad_third = back_product(grad_hidden, full[4])
    unused_third, pull_third = jax.vjp(layer_norm, middle, gain[2], shift[2])
    grad_inner, gain_third, shift_third = pull_third(grad_third)
    grad_middle = cotangent + grad_inner
    unused_branch, pull_branch = jax.vjp(layer_norm, branch, gain[1], shift[1])
    grad_branch, gain_branch, shift_branch = pull_branch(grad_middle)
    grad_branch = grad_branch.astype(jnp.bfloat16)
    grad_out = weight_grad(mixed, grad_branch)
    bias_out = column_sum(grad_branch)
    grad_mixed = back_product(grad_branch, full[3]).astype(jnp.bfloat16)
    grad_qkv = attention_back(qkv, top, logsum, grad_mixed, seqs, heads)
    grad_project = weight_grad(first, grad_qkv)
    qkv_sums = column_sum(grad_qkv)
    grad_first = back_product(grad_qkv, full[2])
    unused_first, pull_first = jax.vjp(layer_norm, block_value, gain[0], shift[0])
    grad_block, gain_first, shift_first = pull_first(grad_first)
    grad_input = grad_middle + grad_block
    grad_gain = jnp.stack([gain_first, gain_branch, gain_third, gain_last])
    grad_shift = jnp.stack([shift_first, shift_branch, shift_third, shift_last])
    grad_bias = jnp.stack([qkv_sums[:width], qkv_sums[2 * width :], bias_out, bias_down])
    return (
        grad_input,
        (grad_gain, grad_shift, grad_project, grad_out, grad_up, grad_down, grad_bias, bias_hidden),
    )


def on_device(
    inputs,
    out_grad,
    group_id,
    group_count,
    norm_gain,
    norm_bias,
    w_qkv,
    w_out,
    w_up,
    w_down,
    bias_model,
    bias_up,
):
    micros, seqs, length, width = inputs.shape
    heads = HEADS
    tokens = seqs * length
    matches = (
        group_id[:, :, None] == jnp.arange(group_count.shape[0], dtype=jnp.int32)[None, None, :]
    )
    counts = jnp.sum(jnp.where(matches, group_count[None, None, :], 0), axis=-1)
    seq_scale = 1.0 / counts.astype(jnp.float32)
    results = []
    grad_inputs = []
    totals = None
    for micro in range(micros):
        full = (
            lax.all_gather(norm_gain, "narrow", axis=1, tiled=True),
            lax.all_gather(norm_bias, "narrow", axis=1, tiled=True),
            lax.all_gather(w_qkv, "narrow", axis=0, tiled=True),
            lax.all_gather(w_out, "narrow", axis=0, tiled=True),
            lax.all_gather(w_up, "narrow", axis=0, tiled=True),
            lax.all_gather(w_down, "narrow", axis=0, tiled=True),
            lax.all_gather(bias_model, "narrow", axis=1, tiled=True),
            lax.all_gather(bias_up, "narrow", axis=0, tiled=True),
        )
        result, kept = forward_pass(inputs[micro].reshape(tokens, width), full, seqs, heads)
        results.append(result.reshape(seqs, length, width).astype(jnp.bfloat16))
        full = (
            lax.all_gather(norm_gain, "narrow", axis=1, tiled=True),
            lax.all_gather(norm_bias, "narrow", axis=1, tiled=True),
            lax.all_gather(w_qkv, "narrow", axis=0, tiled=True),
            lax.all_gather(w_out, "narrow", axis=0, tiled=True),
            lax.all_gather(w_up, "narrow", axis=0, tiled=True),
            lax.all_gather(w_down, "narrow", axis=0, tiled=True),
            lax.all_gather(bias_model, "narrow", axis=1, tiled=True),
            lax.all_gather(bias_up, "narrow", axis=0, tiled=True),
        )
        cotangent = out_grad[micro].astype(jnp.float32) * seq_scale[micro][:, None, None]
        grad_input, grads = backward_pass(cotangent.reshape(tokens, width), full, kept, seqs, heads)
        grad_inputs.append(grad_input.reshape(seqs, length, width).astype(jnp.bfloat16))
        shares = (
            lax.psum_scatter(
                grads[0].astype(jnp.bfloat16), "narrow", scatter_dimension=1, tiled=True
            ).astype(jnp.float32),
            lax.psum_scatter(
                grads[1].astype(jnp.bfloat16), "narrow", scatter_dimension=1, tiled=True
            ).astype(jnp.float32),
            lax.psum_scatter(
                grads[2].astype(jnp.bfloat16), "narrow", scatter_dimension=0, tiled=True
            ).astype(jnp.float32),
            lax.psum_scatter(
                grads[3].astype(jnp.bfloat16), "narrow", scatter_dimension=0, tiled=True
            ).astype(jnp.float32),
            lax.psum_scatter(
                grads[4].astype(jnp.bfloat16), "narrow", scatter_dimension=0, tiled=True
            ).astype(jnp.float32),
            lax.psum_scatter(
                grads[5].astype(jnp.bfloat16), "narrow", scatter_dimension=0, tiled=True
            ).astype(jnp.float32),
            lax.psum_scatter(
                grads[6].astype(jnp.bfloat16), "narrow", scatter_dimension=1, tiled=True
            ).astype(jnp.float32),
            lax.psum_scatter(
                grads[7].astype(jnp.bfloat16), "narrow", scatter_dimension=0, tiled=True
            ).astype(jnp.float32),
        )
        if totals is None:
            totals = tuple(shares)
        else:
            totals = tuple((left + right for left, right in zip(totals, shares)))
    summed = (
        lax.psum(totals[0].astype(jnp.bfloat16), "wide").astype(jnp.float32),
        lax.psum(totals[1].astype(jnp.bfloat16), "wide").astype(jnp.float32),
        lax.psum(totals[2].astype(jnp.bfloat16), "wide").astype(jnp.float32),
        lax.psum(totals[3].astype(jnp.bfloat16), "wide").astype(jnp.float32),
        lax.psum(totals[4].astype(jnp.bfloat16), "wide").astype(jnp.float32),
        lax.psum(totals[5].astype(jnp.bfloat16), "wide").astype(jnp.float32),
        lax.psum(totals[6].astype(jnp.bfloat16), "wide").astype(jnp.float32),
        lax.psum(totals[7].astype(jnp.bfloat16), "wide").astype(jnp.float32),
    )
    output = jnp.stack(results)
    grad_all = jnp.stack(grad_inputs)
    return (
        output,
        grad_all,
        summed[0],
        summed[1],
        summed[2],
        summed[3],
        summed[4],
        summed[5],
        summed[6],
        summed[7],
    )


def solution(mesh):
    return jax.shard_map(
        on_device,
        mesh=mesh,
        in_specs=(
            P(None, ("wide", "narrow"), None, None),
            P(None, ("wide", "narrow"), None, None),
            P(None, ("wide", "narrow")),
            P(),
            P(None, "narrow"),
            P(None, "narrow"),
            P("narrow", None),
            P("narrow", None),
            P("narrow", None),
            P("narrow", None),
            P(None, "narrow"),
            P("narrow"),
        ),
        out_specs=(
            P(None, ("wide", "narrow"), None, None),
            P(None, ("wide", "narrow"), None, None),
            P(None, "narrow"),
            P(None, "narrow"),
            P("narrow", None),
            P("narrow", None),
            P("narrow", None),
            P("narrow", None),
            P(None, "narrow"),
            P("narrow"),
        ),
        check_vma=False,
    )
```

profile of v0, /device:TPU:0, one launch (start us, length us, event | category | flops | bytes accessed | tf_op | source)
XLA Modules:
  0.0 1364.5 jit_solution(11387868374793793821)
XLA Ops:
  10.1 5.3 all_gather.19
  15.4 4.4 all_gather.22
  19.8 4.4 all_gather.17
  24.2 4.6 all_gather.16
  30.1 62.6 %all-gather.5.cloned.1.call-done = bf16[1024,3072]{1,0:T(8,128)(2,1)} async-done(((bf16[512,3072]{1,0:T(8,128)(2,1)}), bf16[1024,3072]{1,0:T(8,128)(2,1)}) %all-gather.5.cloned.1.call-update) | async-done | bytes 6291472 | tf_op jit(solution)/shard_map/all_gather | solution.py:199
  92.7 3.9 fusion.2
  97.0 4.2 fusion.3
  104.4 23.1 %all-gather.7.cloned.1.call-done = bf16[1024,1024]{1,0:T(8,128)(2,1)} async-done(((bf16[512,1024]{1,0:T(8,128)(2,1)}), bf16[1024,1024]{1,0:T(8,128)(2,1)}) %all-gather.7.cloned.1.call-update) | async-done | bytes 2097168 | tf_op jit(solution)/shard_map/all_gather | solution.py:200
  138.8 94.2 %all-gather.9.cloned.1.call-done = bf16[1024,4096]{1,0:T(8,128)(2,1)} async-done(((bf16[512,4096]{1,0:T(8,128)(2,1)}), bf16[1024,4096]{1,0:T(8,128)(2,1)}) %all-gather.9.cloned.1.call-update) | async-done | bytes 8388624 | tf_op jit(solution)/shard_map/all_gather | solution.py:201
  233.0 9.9 multiply_convert_fusion
  242.9 95.5 %all-gather.11.cloned.1.call-done = bf16[4096,1024]{1,0:T(8,128)(2,1)} async-done(((bf16[2048,1024]{1,0:T(8,128)(2,1)}), bf16[4096,1024]{1,0:T(8,128)(2,1)}) %all-gather.11.cloned.1.call-update) | async-done | bytes 8388624 | tf_op jit(solution)/shard_map/all_gather | solution.py:202
  338.4 5.2 fusion.153
  344.5 9.1 multiply_convert_fusion.1
  360.7 5.7 fusion.126
  366.5 2.9 fusion.155
  369.4 5.7 fusion.125
  376.0 3.6 multiply_reduce_fusion.4
  388.1 3.0 convolution_convert_fusion.7
  395.5 2.9 convolution_bitcast_fusion
  402.8 4.7 convolution_convert_fusion.4
  414.4 4.6 convolution_convert_fusion.5
  420.1 7.1 convolution_convert_fusion.2
  427.2 7.2 convolution_convert_fusion.3
  435.7 5.6 convolution_convert_fusion
  442.6 5.6 convolution_convert_fusion.1
  450.7 5.1 fusion.156
  455.7 5.1 fusion.53
  468.0 2.9 add_convert_fusion.3
  470.9 62.1 %reduce-scatter.29.cloned.1.call-done = bf16[512,3072]{1,0:T(8,128)(2,1)} async-done(((bf16[1024,3072]{1,0:T(8,128)(2,1)}), bf16[512,3072]{1,0:T(8,128)(2,1)}) %reduce-scatter.29.cloned.1.call-update) | async-done | bytes 3145744 | tf_op jit(solution)/shard_map/reduce_scatter | solution.py:228
  533.0 79.5 %reduce-scatter.27.cloned.1.call-done = bf16[512,3072]{1,0:T(8,128)(2,1)} async-done(((bf16[1024,3072]{1,0:T(8,128)(2,1)}), bf16[512,3072]{1,0:T(8,128)(2,1)}) %reduce-scatter.27.cloned.1.call-update) | async-done | bytes 3145744 | tf_op jit(solution)/shard_map/reduce_scatter | solution.py:228
  612.5 5.7 add_convert_fusion.2
  618.2 96.6 %reduce-scatter.37.cloned.1.call-done = bf16[512,4096]{1,0:T(8,128)(2,1)} async-done(((bf16[1024,4096]{1,0:T(8,128)(2,1)}), bf16[512,4096]{1,0:T(8,128)(2,1)}) %reduce-scatter.37.cloned.1.call-update) | async-done | bytes 4194320 | tf_op jit(solution)/shard_map/reduce_scatter | solution.py:234
  714.7 102.1 %reduce-scatter.35.cloned.1.call-done = bf16[512,4096]{1,0:T(8,128)(2,1)} async-done(((bf16[1024,4096]{1,0:T(8,128)(2,1)}), bf16[512,4096]{1,0:T(8,128)(2,1)}) %reduce-scatter.35.cloned.1.call-update) | async-done | bytes 4194320 | tf_op jit(solution)/shard_map/reduce_scatter | solution.py:234
  816.8 7.2 add_convert_fusion.1
  824.1 94.4 %reduce-scatter.41.cloned.1.call-done = bf16[2048,1024]{1,0:T(8,128)(2,1)} async-done(((bf16[4096,1024]{1,0:T(8,128)(2,1)}), bf16[2048,1024]{1,0:T(8,128)(2,1)}) %reduce-scatter.41.cloned.1.call-update) | async-done | bytes 4194320 | tf_op jit(solution)/shard_map/reduce_scatter | solution.py:237
  918.5 101.5 %reduce-scatter.39.cloned.1.call-done = bf16[2048,1024]{1,0:T(8,128)(2,1)} async-done(((bf16[4096,1024]{1,0:T(8,128)(2,1)}), bf16[2048,1024]{1,0:T(8,128)(2,1)}) %reduce-scatter.39.cloned.1.call-update) | async-done | bytes 4194320 | tf_op jit(solution)/shard_map/reduce_scatter | solution.py:237
  1020.0 7.6 add_convert_fusion
  1029.5 6.9 all-reduce.4
  1039.5 8.4 reduce-scatter.43.cloned.1.call-done
  1048.9 12.9 reduce-scatter.49.cloned.1.call-done
  1062.8 12.9 reduce-scatter.47.cloned.1.call-done
  1076.7 12.9 reduce-scatter.53.cloned.1.call-done
  1090.5 12.9 reduce-scatter.51.cloned.1.call-done
  1104.5 64.5 %all-reduce.2 = (bf16[4,512]{1,0:T(4,128)(2,1)S(1)}, bf16[4,512]{1,0:T(4,128)(2,1)S(1)}, bf16[4,512]{1,0:T(4,128)(2,1)S(1)}, bf16[2048]{0:T(1024)(128)(2,1)S(1)}) all-reduce(bf16[4,512]{1,0:T(4,128)(2,1)S(1)} %add_convert_fusion.19, bf16[4,512]{1,0:T(4,128)(2,1)S(1)} %add_convert_fusion.18, ...), channel_id=1, replica_groups=mesh['wide'=16,'narrow'=2] {'wide'}, use_global_device_ids=true, to_apply=%region_49.50 | all-reduce | flops 8192 | bytes 32768 | tf_op jit(solution)/shard_map/psum | solution.py:252
  1171.4 170.0 %all-reduce.7.cloned.1.call-done = (bf16[512,3072]{1,0:T(8,128)(2,1)}, bf16[512,1024]{1,0:T(8,128)(2,1)}, bf16[512,4096]{1,0:T(8,128)(2,1)}, bf16[2048,1024]{1,0:T(8,128)(2,1)}) async-done(((bf16[512,3072]{1,0:T(8,128)(2,1)}, bf16[512,1024]{1,0:T(8,128)(2,1)}, bf16[512,4096]{1,0:T(8,128)(2,1)}, bf16[2048,1024]{1,0:T(8,128)(2,1)}), (bf16[512,3072]{1,0:T(8,128)(2,1)}, bf16[512,1024]{1,0:T(8,128)(2,1)}, ...) | async-done | bytes 12582928 | tf_op jit(solution)/shard_map/psum | solution.py:254
  1341.4 5.5 convert_element_type.454
  1348.6 4.5 convert_element_type.466
  1353.0 4.4 convert_element_type.472
  (319 shorter events, 77.8 us)
Async XLA Ops:
  7.2 85.5 %all-gather.5.cloned.1.call-start = ((), (), s32[]{:S(2)}) async-start(), calls=%async_computation.14 | async-start | bytes 9437184 | tf_op jit(solution)/shard_map/all_gather | solution.py:199
  7.9 119.5 %all-gather.7.cloned.1.call-start = ((), (), s32[]{:S(2)}) async-start(), calls=%async_computation.15 | async-start | bytes 3145728 | tf_op jit(solution)/shard_map/all_gather | solution.py:200
  8.7 224.3 %all-gather.9.cloned.1.call-start = ((), (), s32[]{:S(2)}) async-start(), calls=%async_computation.16 | async-start | bytes 12582912 | tf_op jit(solution)/shard_map/all_gather | solution.py:201
  9.4 6.0 copy-start.47
  9.4 10.4 copy-start.48
  9.4 14.7 %copy-start.49 = (bf16[4,512]{1,0:T(4,128)(2,1)S(1)}, bf16[4,512]{1,0:T(4,128)(2,1)}, u32[]{:S(2)}) copy-start(bf16[4,512]{1,0:T(4,128)(2,1)} %param.16) | copy-start | bytes 12292
  9.4 19.3 %copy-start.2 = (bf16[2,1,128,1024]{3,2,1,0:T(8,128)(2,1)S(1)}, bf16[2,1,128,1024]{3,2,1,0:T(8,128)(2,1)}, u32[]{:S(2)}) copy-start(bf16[2,1,128,1024]{3,2,1,0:T(8,128)(2,1)} %param.12) | copy-start | bytes 1572868
  9.4 19.4 %copy-start.60 = (s32[16]{0:T(128)S(1)}, s32[16]{0:T(128)}, u32[]{:S(2)}) copy-start(s32[16]{0:T(128)} %param.15) | copy-start | bytes 196
  9.5 19.4 %copy-start.61 = (s32[2,1]{0,1:T(1,128)S(1)}, s32[2,1]{0,1:T(1,128)}, u32[]{:S(2)}) copy-start(s32[2,1]{0,1:T(1,128)} %param.14) | copy-start | bytes 28
  9.5 328.9 %all-gather.11.cloned.1.call-start = ((), (), s32[]{:S(2)}) async-start(), calls=%async_computation.17 | async-start | bytes 12582912 | tf_op jit(solution)/shard_map/all_gather | solution.py:202
  10.0 457.9 %reduce-scatter.33.cloned.1.call-start = ((), (), s32[]{:S(2)}) async-start(), calls=%async_computation.21 | async-start | bytes 3145728 | tf_op jit(solution)/shard_map/reduce_scatter | solution.py:231
  29.4 67.2 %copy-start.52 = (f32[128]{0:T(128)}, f32[128]{0:T(128)S(1)}, u32[]{:S(2)}) copy-start(f32[128]{0:T(128)S(1)} %get-tuple-element.41) | copy-start | bytes 1540
  96.9 6.4 copy-start.18
  101.5 30.6 %copy-start.20 = (bf16[128,3072]{0,1:T(8,128)(2,1)}, bf16[128,3072]{0,1:T(8,128)(2,1)S(1)}, u32[]{:S(2)}) copy-start(bf16[128,3072]{0,1:T(8,128)(2,1)S(1)} %copy.66) | copy-start | bytes 2359300
  104.4 27.7 %copy-start.34 = (bf16[16,64,128]{2,1,0:T(8,128)(2,1)}, bf16[16,64,128]{2,1,0:T(8,128)(2,1)S(1)}, u32[]{:S(2)}) copy-start(bf16[16,64,128]{2,1,0:T(8,128)(2,1)S(1)} %convolution_convert_fusion.11) | copy-start | bytes 786436
  130.6 6.5 copy-start.54
  137.0 105.9 %copy-start.56 = (f32[128]{0:T(128)}, f32[128]{0:T(128)S(1)}, u32[]{:S(2)}) copy-start(f32[128]{0:T(128)S(1)} %multiply_reduce_fusion.14) | copy-start | bytes 1540
  138.8 104.2 %copy-start.58 = (f32[128]{0:T(128)}, f32[128]{0:T(128)S(1)}, u32[]{:S(2)}) copy-start(f32[128]{0:T(128)S(1)} %multiply_reduce_fusion.16) | copy-start | bytes 1540
  338.4 6.1 copy-start.1
  338.4 16.2 %slice-start = ((s8[8388608]{0:T(1024)(128)(4,1)}), s8[4194304]{0:T(1024)(128)(4,1)S(1)}, s32[]{:S(2)}) async-start(s8[8388608]{0:T(1024)(128)(4,1)} %bitcast.286), calls=%async_computation.33 | async-start | bytes 8388608
  344.5 10.1 slice-start.1
  360.6 5.9 copy-start.40
  360.7 8.7 copy-start.38
  376.0 3.8 copy-start.59
  386.9 81.1 %reduce-scatter.31.cloned.1.call-start = ((), (), s32[]{:S(2)}) async-start(), calls=%async_computation.20 | async-start | bytes 3145728 | tf_op jit(solution)/shard_map/reduce_scatter | solution.py:231
  391.1 141.9 %reduce-scatter.29.cloned.1.call-start = ((), (), s32[]{:S(2)}) async-start(), calls=%async_computation.19 | async-start | bytes 9437184 | tf_op jit(solution)/shard_map/reduce_scatter | solution.py:228
  407.5 205.0 %reduce-scatter.27.cloned.1.call-start = ((), (), s32[]{:S(2)}) async-start(), calls=%async_computation.18 | async-start | bytes 9437184 | tf_op jit(solution)/shard_map/reduce_scatter | solution.py:228
  419.1 295.7 %reduce-scatter.37.cloned.1.call-start = ((), (), s32[]{:S(2)}) async-start(), calls=%async_computation.23 | async-start | bytes 12582912 | tf_op jit(solution)/shard_map/reduce_scatter | solution.py:234
  427.2 389.6 %reduce-scatter.35.cloned.1.call-start = ((), (), s32[]{:S(2)}) async-start(), calls=%async_computation.22 | async-start | bytes 12582912 | tf_op jit(solution)/shard_map/reduce_scatter | solution.py:234
  434.5 484.0 %reduce-scatter.41.cloned.1.call-start = ((), (), s32[]{:S(2)}) async-start(), calls=%async_computation.25 | async-start | bytes 12582912 | tf_op jit(solution)/shard_map/reduce_scatter | solution.py:237
  441.3 578.7 %reduce-scatter.39.cloned.1.call-start = ((), (), s32[]{:S(2)}) async-start(), calls=%async_computation.24 | async-start | bytes 12582912 | tf_op jit(solution)/shard_map/reduce_scatter | solution.py:237
  448.2 590.3 %reduce-scatter.45.cloned.1.call-start = ((), (), s32[]{:S(2)}) async-start(), calls=%async_computation.27 | async-start | bytes 393216
  455.7 5.1 copy-start.53
  455.7 5.2 copy-start.51
  455.7 6.7 copy-start.45
  462.5 585.4 %reduce-scatter.43.cloned.1.call-start = ((), (), s32[]{:S(2)}) async-start(), calls=%async_computation.26 | async-start | bytes 393216
  463.5 598.3 %reduce-scatter.49.cloned.1.call-start = ((), (), s32[]{:S(2)}) async-start(), calls=%async_computation.29 | async-start | bytes 393216
  464.5 611.1 %reduce-scatter.47.cloned.1.call-start = ((), (), s32[]{:S(2)}) async-start(), calls=%async_computation.28 | async-start | bytes 393216
  465.7 623.8 %reduce-scatter.53.cloned.1.call-start = ((), (), s32[]{:S(2)}) async-start(), calls=%async_computation.31 | async-start | bytes 393216
  466.9 636.5 %reduce-scatter.51.cloned.1.call-start = ((), (), s32[]{:S(2)}) async-start(), calls=%async_computation.30 | async-start | bytes 393216
  467.9 873.5 %all-reduce.7.cloned.1.call-start = ((), (), s32[]{:S(2)}) async-start(), calls=%async_computation.32 | async-start | bytes 25165824 | tf_op jit(solution)/shard_map/psum | solution.py:254
  1027.6 8.8 copy-start.36
  1027.6 8.8 copy-start.37
  1027.6 9.7 copy-start.23
  1027.6 9.7 copy-start.25
  1341.4 5.5 copy-start.33
  1341.4 7.1 copy-start.27
  1348.5 4.5 copy-start.26
  (36 other events, 58.3 us)
Sparse Core Ops, SparseCore 0:
  9.5 83.1 all-gather.4
  94.2 33.1 all-gather.6
  129.0 103.9 all-gather.8
  234.4 103.9 all-gather.10
  387.0 31.8 reduce-scatter.32
  421.0 31.8 reduce-scatter.30
  455.8 77.1 reduce-scatter.28
  535.3 77.1 reduce-scatter.26
  615.4 99.3 reduce-scatter.36
  717.4 99.3 reduce-scatter.34
  819.1 99.3 reduce-scatter.40
  920.6 99.3 reduce-scatter.38
  1022.2 11.7 reduce-scatter.44
  1036.1 11.7 reduce-scatter.42
  1050.0 11.7 reduce-scatter.48
  1063.9 11.7 reduce-scatter.46
  1077.7 11.7 reduce-scatter.52
  1091.6 11.7 reduce-scatter.50
  1108.6 232.8 all-reduce.6
where the time goes:
time: 1370 us; the launch traced here: 1360 us
  waiting for transfers between devices  1040 us (76%)
  matrix products  125 us (9%)
  blocking collectives  90 us (7%)
  other arithmetic  59 us (4%)
  local copies, waits for them, and re-layouts  28.8 us (2%)
  between operations  16.4 us (1%)
    reduce_scatter x2, waiting for transfers between devices, on_device(): lax.psum_scatter(grads[4].astype(jnp.bfloat16), 'narrow', scatter_dimensi...  199 us
    reduce_scatter x2, waiting for transfers between devices, on_device(): lax.psum_scatter(grads[5].astype(jnp.bfloat16), 'narrow', scatter_dimensi...  196 us
    psum x1, waiting for transfers between devices, on_device(): lax.psum(totals[2].astype(jnp.bfloat16), 'wide').astype(jnp.float32)  170 us
    reduce_scatter x2, waiting for transfers between devices, on_device(): lax.psum_scatter(grads[2].astype(jnp.bfloat16), 'narrow', scatter_dimensi...  142 us
    all_gather x1, waiting for transfers between devices, on_device(): lax.all_gather(w_down, 'narrow', axis=0, tiled=True)  95.5 us
    all_gather x1, waiting for transfers between devices, on_device(): lax.all_gather(w_up, 'narrow', axis=0, tiled=True)  94.2 us
    psum x1, blocking collectives, on_device(): lax.psum(totals[0].astype(jnp.bfloat16), 'wide').astype(jnp.float32)  64.5 us
    unnamed x25, waiting for transfers between devices  62.7 us
  transfers between devices with their start and end apart: 19, of which 16 were waited for; matrix products, arithmetic and copies ran while one was open for 10% of the time, Pallas kernels for 0%

commit v1 on v0

--- a/solution.py
+++ b/solution.py
@@ -249,7 +249,7 @@
         else:
             totals = tuple((left + right for left, right in zip(totals, shares)))
     summed = (
-        lax.psum(totals[0].astype(jnp.bfloat16), "wide").astype(jnp.float32),
+        jnp.sum(lax.all_gather(totals[0].astype(jnp.bfloat16), "wide"), axis=0).astype(jnp.float32),
         lax.psum(totals[1].astype(jnp.bfloat16), "wide").astype(jnp.float32),
         lax.psum(totals[2].astype(jnp.bfloat16), "wide").astype(jnp.float32),
         lax.psum(totals[3].astype(jnp.bfloat16), "wide").astype(jnp.float32),

time: 1370 us -> 1370 us (level)
  blocking collectives: 90 us -> 111 us
  waiting for transfers between devices: 1040 us -> 1020 us
    unnamed x25, waiting for transfers between devices: 62.7 us -> 40.6 us
    all_gather x0 -> x1, blocking collectives: none -> 21.5 us  [on_device(): lax.all_gather(totals[0].astype(jnp.bfloat16), 'wide')]
  transfers between devices with their start and end apart: 19 -> 19, of which waited for: 16 -> 15; matrix products, arithmetic and copies ran while one was open for 10% -> 10% of each run, Pallas kernels for 0% -> 0%
where the time goes in v1:
time: 1370 us; the launch traced here: 1360 us
  waiting for transfers between devices  1020 us (74%)
  matrix products  125 us (9%)
  blocking collectives  111 us (8%)
  other arithmetic  59.1 us (4%)
  local copies, waits for them, and re-layouts  28.7 us (2%)
  between operations  16.1 us (1%)
    reduce_scatter x2, waiting for transfers between devices, on_device(): lax.psum_scatter(grads[4].astype(jnp.bfloat16), 'narrow', scatter_dimensi...  199 us
    reduce_scatter x2, waiting for transfers between devices, on_device(): lax.psum_scatter(grads[5].astype(jnp.bfloat16), 'narrow', scatter_dimensi...  196 us
    psum x1, waiting for transfers between devices, on_device(): lax.psum(totals[2].astype(jnp.bfloat16), 'wide').astype(jnp.float32)  171 us
    reduce_scatter x2, waiting for transfers between devices, on_device(): lax.psum_scatter(grads[2].astype(jnp.bfloat16), 'narrow', scatter_dimensi...  142 us
    all_gather x1, waiting for transfers between devices, on_device(): lax.all_gather(w_down, 'narrow', axis=0, tiled=True)  95.4 us
    all_gather x1, waiting for transfers between devices, on_device(): lax.all_gather(w_up, 'narrow', axis=0, tiled=True)  94.2 us
    psum x1, blocking collectives, on_device(): lax.psum(totals[1].astype(jnp.bfloat16), 'wide').astype(jnp.float32)  64.3 us
    all_gather x1, waiting for transfers between devices, on_device(): lax.all_gather(w_qkv, 'narrow', axis=0, tiled=True)  62.6 us
  transfers between devices with their start and end apart: 19, of which 15 were waited for; matrix products, arithmetic and copies ran while one was open for 10% of the time, Pallas kernels for 0%

profile of v1, /device:TPU:0, one launch (start us, length us, event | category | flops | bytes accessed | tf_op | source)
XLA Modules:
  0.0 1364.3 jit_solution(12463062883724009330)
XLA Ops:
  10.1 5.3 all_gather.23
  15.4 4.4 all_gather.26
  19.8 4.4 all_gather.21
  24.2 4.6 all_gather.20
  30.1 62.6 %all-gather.7.cloned.1.call-done = bf16[1024,3072]{1,0:T(8,128)(2,1)} async-done(((bf16[512,3072]{1,0:T(8,128)(2,1)}), bf16[1024,3072]{1,0:T(8,128)(2,1)}) %all-gather.7.cloned.1.call-update) | async-done | bytes 6291472 | tf_op jit(solution)/shard_map/all_gather | solution.py:199
  92.7 3.9 fusion.2
  97.0 4.2 fusion.3
  104.4 23.1 %all-gather.9.cloned.1.call-done = bf16[1024,1024]{1,0:T(8,128)(2,1)} async-done(((bf16[512,1024]{1,0:T(8,128)(2,1)}), bf16[1024,1024]{1,0:T(8,128)(2,1)}) %all-gather.9.cloned.1.call-update) | async-done | bytes 2097168 | tf_op jit(solution)/shard_map/all_gather | solution.py:200
  138.8 94.2 %all-gather.11.cloned.1.call-done = bf16[1024,4096]{1,0:T(8,128)(2,1)} async-done(((bf16[512,4096]{1,0:T(8,128)(2,1)}), bf16[1024,4096]{1,0:T(8,128)(2,1)}) %all-gather.11.cloned.1.call-update) | async-done | bytes 8388624 | tf_op jit(solution)/shard_map/all_gather | solution.py:201
  233.0 10.0 multiply_convert_fusion
  243.0 95.4 %all-gather.13.cloned.1.call-done = bf16[4096,1024]{1,0:T(8,128)(2,1)} async-done(((bf16[2048,1024]{1,0:T(8,128)(2,1)}), bf16[4096,1024]{1,0:T(8,128)(2,1)}) %all-gather.13.cloned.1.call-update) | async-done | bytes 8388624 | tf_op jit(solution)/shard_map/all_gather | solution.py:202
  338.4 5.2 fusion.154
  344.5 9.2 multiply_convert_fusion.1
  360.9 5.7 fusion.127
  366.6 2.9 fusion.156
  369.5 5.7 fusion.126
  376.2 3.6 multiply_reduce_fusion.4
  388.2 3.0 convolution_convert_fusion.7
  395.6 2.9 convolution_bitcast_fusion
  402.9 4.7 convolution_convert_fusion.4
  414.5 4.6 convolution_convert_fusion.5
  420.2 7.1 convolution_convert_fusion.2
  427.4 7.2 convolution_convert_fusion.3
  435.8 5.6 convolution_convert_fusion
  442.7 5.6 convolution_convert_fusion.1
  450.8 5.1 fusion.157
  455.9 5.1 fusion.53
  468.1 2.9 add_convert_fusion.3
  471.0 62.1 %reduce-scatter.29.cloned.1.call-done = bf16[512,3072]{1,0:T(8,128)(2,1)} async-done(((bf16[1024,3072]{1,0:T(8,128)(2,1)}), bf16[512,3072]{1,0:T(8,128)(2,1)}) %reduce-scatter.29.cloned.1.call-update) | async-done | bytes 3145744 | tf_op jit(solution)/shard_map/reduce_scatter | solution.py:228
  533.1 79.5 %reduce-scatter.27.cloned.1.call-done = bf16[512,3072]{1,0:T(8,128)(2,1)} async-done(((bf16[1024,3072]{1,0:T(8,128)(2,1)}), bf16[512,3072]{1,0:T(8,128)(2,1)}) %reduce-scatter.27.cloned.1.call-update) | async-done | bytes 3145744 | tf_op jit(solution)/shard_map/reduce_scatter | solution.py:228
  612.6 5.7 add_convert_fusion.2
  618.3 96.6 %reduce-scatter.37.cloned.1.call-done = bf16[512,4096]{1,0:T(8,128)(2,1)} async-done(((bf16[1024,4096]{1,0:T(8,128)(2,1)}), bf16[512,4096]{1,0:T(8,128)(2,1)}) %reduce-scatter.37.cloned.1.call-update) | async-done | bytes 4194320 | tf_op jit(solution)/shard_map/reduce_scatter | solution.py:234
  714.9 102.1 %reduce-scatter.35.cloned.1.call-done = bf16[512,4096]{1,0:T(8,128)(2,1)} async-done(((bf16[1024,4096]{1,0:T(8,128)(2,1)}), bf16[512,4096]{1,0:T(8,128)(2,1)}) %reduce-scatter.35.cloned.1.call-update) | async-done | bytes 4194320 | tf_op jit(solution)/shard_map/reduce_scatter | solution.py:234
  816.9 7.2 add_convert_fusion.1
  824.2 94.4 %reduce-scatter.41.cloned.1.call-done = bf16[2048,1024]{1,0:T(8,128)(2,1)} async-done(((bf16[4096,1024]{1,0:T(8,128)(2,1)}), bf16[2048,1024]{1,0:T(8,128)(2,1)}) %reduce-scatter.41.cloned.1.call-update) | async-done | bytes 4194320 | tf_op jit(solution)/shard_map/reduce_scatter | solution.py:237
  918.6 101.5 %reduce-scatter.39.cloned.1.call-done = bf16[2048,1024]{1,0:T(8,128)(2,1)} async-done(((bf16[4096,1024]{1,0:T(8,128)(2,1)}), bf16[2048,1024]{1,0:T(8,128)(2,1)}) %reduce-scatter.39.cloned.1.call-update) | async-done | bytes 4194320 | tf_op jit(solution)/shard_map/reduce_scatter | solution.py:237
  1020.1 7.6 add_convert_fusion
  1029.6 6.9 all-reduce.4
  1039.7 8.4 reduce-scatter.43.cloned.1.call-done
  1049.0 21.5 %all-gather.1 = bf16[16,4,512]{2,1,0:T(4,128)(2,1)S(1)} all-gather(bf16[1,4,512]{2,1,0:T(4,128)(2,1)S(1)} %fusion.102), channel_id=2, replica_groups=mesh['wide'=16,'narrow'=2] {'wide'}, dimensions={0}, use_global_device_ids=true | all-gather | bytes 69632 | tf_op jit(solution)/shard_map/all_gather | solution.py:252
  1072.2 3.6 reduce-scatter.47.cloned.1.call-done
  1076.8 12.9 reduce-scatter.53.cloned.1.call-done
  1090.7 12.9 reduce-scatter.51.cloned.1.call-done
  1104.6 64.3 %all-reduce.2 = (bf16[4,512]{1,0:T(4,128)(2,1)S(1)}, bf16[4,512]{1,0:T(4,128)(2,1)S(1)}, bf16[2048]{0:T(1024)(128)(2,1)S(1)}) all-reduce(bf16[4,512]{1,0:T(4,128)(2,1)S(1)} %add_convert_fusion.18, bf16[4,512]{1,0:T(4,128)(2,1)S(1)} %add_convert_fusion.17, ...), channel_id=1, replica_groups=mesh['wide'=16,'narrow'=2] {'wide'}, use_global_device_ids=true, to_apply=%region_60.61 | all-reduce | flops 6144 | bytes 24576 | tf_op jit(solution)/shard_map/psum | solution.py:253
  1170.6 170.9 %all-reduce.7.cloned.1.call-done = (bf16[512,3072]{1,0:T(8,128)(2,1)}, bf16[512,1024]{1,0:T(8,128)(2,1)}, bf16[512,4096]{1,0:T(8,128)(2,1)}, bf16[2048,1024]{1,0:T(8,128)(2,1)}) async-done(((bf16[512,3072]{1,0:T(8,128)(2,1)}, bf16[512,1024]{1,0:T(8,128)(2,1)}, bf16[512,4096]{1,0:T(8,128)(2,1)}, bf16[2048,1024]{1,0:T(8,128)(2,1)}), (bf16[512,3072]{1,0:T(8,128)(2,1)}, bf16[512,1024]{1,0:T(8,128)(2,1)}, ...) | async-done | bytes 12582928 | tf_op jit(solution)/shard_map/psum | solution.py:254
  1341.6 5.5 convert_element_type.456
  1348.7 4.5 convert_element_type.468
  1353.2 4.4 convert_element_type.474
  (321 shorter events, 77.8 us)
Async XLA Ops:
  7.2 85.5 %all-gather.7.cloned.1.call-start = ((), (), s32[]{:S(2)}) async-start(), calls=%async_computation.14 | async-start | bytes 9437184 | tf_op jit(solution)/shard_map/all_gather | solution.py:199
  7.9 119.5 %all-gather.9.cloned.1.call-start = ((), (), s32[]{:S(2)}) async-start(), calls=%async_computation.15 | async-start | bytes 3145728 | tf_op jit(solution)/shard_map/all_gather | solution.py:200
  8.7 224.3 %all-gather.11.cloned.1.call-start = ((), (), s32[]{:S(2)}) async-start(), calls=%async_computation.16 | async-start | bytes 12582912 | tf_op jit(solution)/shard_map/all_gather | solution.py:201
  9.4 6.0 copy-start.47
  9.4 10.4 copy-start.48
  9.4 14.7 %copy-start.49 = (bf16[4,512]{1,0:T(4,128)(2,1)S(1)}, bf16[4,512]{1,0:T(4,128)(2,1)}, u32[]{:S(2)}) copy-start(bf16[4,512]{1,0:T(4,128)(2,1)} %param.16) | copy-start | bytes 12292
  9.4 19.3 %copy-start.2 = (bf16[2,1,128,1024]{3,2,1,0:T(8,128)(2,1)S(1)}, bf16[2,1,128,1024]{3,2,1,0:T(8,128)(2,1)}, u32[]{:S(2)}) copy-start(bf16[2,1,128,1024]{3,2,1,0:T(8,128)(2,1)} %param.12) | copy-start | bytes 1572868
  9.4 19.4 %copy-start.60 = (s32[16]{0:T(128)S(1)}, s32[16]{0:T(128)}, u32[]{:S(2)}) copy-start(s32[16]{0:T(128)} %param.15) | copy-start | bytes 196
  9.5 19.4 %copy-start.61 = (s32[2,1]{0,1:T(1,128)S(1)}, s32[2,1]{0,1:T(1,128)}, u32[]{:S(2)}) copy-start(s32[2,1]{0,1:T(1,128)} %param.14) | copy-start | bytes 28
  9.5 328.9 %all-gather.13.cloned.1.call-start = ((), (), s32[]{:S(2)}) async-start(), calls=%async_computation.17 | async-start | bytes 12582912 | tf_op jit(solution)/shard_map/all_gather | solution.py:202
  10.0 458.0 %reduce-scatter.33.cloned.1.call-start = ((), (), s32[]{:S(2)}) async-start(), calls=%async_computation.21 | async-start | bytes 3145728 | tf_op jit(solution)/shard_map/reduce_scatter | solution.py:231
  29.4 67.2 %copy-start.52 = (f32[128]{0:T(128)}, f32[128]{0:T(128)S(1)}, u32[]{:S(2)}) copy-start(f32[128]{0:T(128)S(1)} %get-tuple-element.41) | copy-start | bytes 1540
  96.9 6.4 copy-start.18
  101.5 30.6 %copy-start.20 = (bf16[128,3072]{0,1:T(8,128)(2,1)}, bf16[128,3072]{0,1:T(8,128)(2,1)S(1)}, u32[]{:S(2)}) copy-start(bf16[128,3072]{0,1:T(8,128)(2,1)S(1)} %copy.66) | copy-start | bytes 2359300
  104.4 27.7 %copy-start.34 = (bf16[16,64,128]{2,1,0:T(8,128)(2,1)}, bf16[16,64,128]{2,1,0:T(8,128)(2,1)S(1)}, u32[]{:S(2)}) copy-start(bf16[16,64,128]{2,1,0:T(8,128)(2,1)S(1)} %convolution_convert_fusion.11) | copy-start | bytes 786436
  130.6 6.5 copy-start.54
  137.0 106.0 %copy-start.56 = (f32[128]{0:T(128)}, f32[128]{0:T(128)S(1)}, u32[]{:S(2)}) copy-start(f32[128]{0:T(128)S(1)} %multiply_reduce_fusion.14) | copy-start | bytes 1540
  138.8 104.3 %copy-start.58 = (f32[128]{0:T(128)}, f32[128]{0:T(128)S(1)}, u32[]{:S(2)}) copy-start(f32[128]{0:T(128)S(1)} %multiply_reduce_fusion.16) | copy-start | bytes 1540
  338.4 6.1 copy-start.1
  338.4 16.3 %slice-start = ((s8[8388608]{0:T(1024)(128)(4,1)}), s8[4194304]{0:T(1024)(128)(4,1)S(1)}, s32[]{:S(2)}) async-start(s8[8388608]{0:T(1024)(128)(4,1)} %bitcast.288), calls=%async_computation.33 | async-start | bytes 8388608
  344.5 10.2 slice-start.1
  360.7 5.9 copy-start.40
  360.9 8.7 copy-start.38
  376.2 3.8 copy-start.59
  387.0 81.1 %reduce-scatter.31.cloned.1.call-start = ((), (), s32[]{:S(2)}) async-start(), calls=%async_computation.20 | async-start | bytes 3145728 | tf_op jit(solution)/shard_map/reduce_scatter | solution.py:231
  391.3 141.9 %reduce-scatter.29.cloned.1.call-start = ((), (), s32[]{:S(2)}) async-start(), calls=%async_computation.19 | async-start | bytes 9437184 | tf_op jit(solution)/shard_map/reduce_scatter | solution.py:228
  407.6 205.0 %reduce-scatter.27.cloned.1.call-start = ((), (), s32[]{:S(2)}) async-start(), calls=%async_computation.18 | async-start | bytes 9437184 | tf_op jit(solution)/shard_map/reduce_scatter | solution.py:228
  419.2 295.7 %reduce-scatter.37.cloned.1.call-start = ((), (), s32[]{:S(2)}) async-start(), calls=%async_computation.23 | async-start | bytes 12582912 | tf_op jit(solution)/shard_map/reduce_scatter | solution.py:234
  427.3 389.6 %reduce-scatter.35.cloned.1.call-start = ((), (), s32[]{:S(2)}) async-start(), calls=%async_computation.22 | async-start | bytes 12582912 | tf_op jit(solution)/shard_map/reduce_scatter | solution.py:234
  434.6 484.0 %reduce-scatter.41.cloned.1.call-start = ((), (), s32[]{:S(2)}) async-start(), calls=%async_computation.25 | async-start | bytes 12582912 | tf_op jit(solution)/shard_map/reduce_scatter | solution.py:237
  441.5 578.7 %reduce-scatter.39.cloned.1.call-start = ((), (), s32[]{:S(2)}) async-start(), calls=%async_computation.24 | async-start | bytes 12582912 | tf_op jit(solution)/shard_map/reduce_scatter | solution.py:237
  448.4 590.3 %reduce-scatter.45.cloned.1.call-start = ((), (), s32[]{:S(2)}) async-start(), calls=%async_computation.27 | async-start | bytes 393216
  455.8 5.1 copy-start.53
  455.9 5.2 copy-start.51
  455.9 6.7 copy-start.45
  462.6 585.4 %reduce-scatter.43.cloned.1.call-start = ((), (), s32[]{:S(2)}) async-start(), calls=%async_computation.26 | async-start | bytes 393216
  463.7 607.5 %reduce-scatter.49.cloned.1.call-start = ((), (), s32[]{:S(2)}) async-start(), calls=%async_computation.29 | async-start | bytes 393216
  464.7 611.1 %reduce-scatter.47.cloned.1.call-start = ((), (), s32[]{:S(2)}) async-start(), calls=%async_computation.28 | async-start | bytes 393216
  465.9 623.8 %reduce-scatter.53.cloned.1.call-start = ((), (), s32[]{:S(2)}) async-start(), calls=%async_computation.31 | async-start | bytes 393216
  467.0 636.5 %reduce-scatter.51.cloned.1.call-start = ((), (), s32[]{:S(2)}) async-start(), calls=%async_computation.30 | async-start | bytes 393216
  468.0 873.6 %all-reduce.7.cloned.1.call-start = ((), (), s32[]{:S(2)}) async-start(), calls=%async_computation.32 | async-start | bytes 25165824 | tf_op jit(solution)/shard_map/psum | solution.py:254
  1027.7 8.8 copy-start.36
  1027.7 8.8 copy-start.37
  1027.7 9.7 copy-start.23
  1027.7 9.7 copy-start.25
  1341.6 5.5 copy-start.33
  1341.6 7.1 copy-start.27
  1348.7 4.5 copy-start.26
  (36 other events, 58.3 us)
Sparse Core Ops, SparseCore 0:
  9.5 83.1 all-gather.6
  94.2 33.1 all-gather.8
  129.0 103.9 all-gather.10
  234.4 103.9 all-gather.12
  387.1 31.8 reduce-scatter.32
  421.2 31.8 reduce-scatter.30
  456.0 77.1 reduce-scatter.28
  535.4 77.1 reduce-scatter.26
  615.5 99.3 reduce-scatter.36
  717.6 99.3 reduce-scatter.34
  819.2 99.3 reduce-scatter.40
  920.7 99.3 reduce-scatter.38
  1022.3 11.7 reduce-scatter.44
  1036.2 11.7 reduce-scatter.42
  1050.1 11.7 reduce-scatter.48
  1064.0 11.7 reduce-scatter.46
  1077.9 11.7 reduce-scatter.52
  1091.7 11.7 reduce-scatter.50
  1108.7 232.8 all-reduce.6
